TPU v7x, 32 devices: a whole 2x2x4 slice. The times are simulated.
32 devices in a mesh: grp: 2 (over x), seq: 8 (over z, y), col: 2 (over core).
Axes of the slice: x: 2, y: 2, z: 4, core: 2. Of those that a mesh axis runs over, the one named last changes fastest.
Arguments:
- signal: bfloat16 [8192, 1408], P(('grp', 'seq'), 'col'), parts along dimension 0, may hold values from -6 to 6
- conv_weight: bfloat16 [5, 1408, 1408], P(None, None, 'col'), may hold values from -0.15625 to 0.15625
- conv_gain: float32 [1408], replicated, may hold values from 0.1 to 1.9
- embed_weight: bfloat16 [1408, 1536], P('col', 'seq'), may hold values from -0.15625 to 0.15625
- attn_gain: float32 [1536], replicated, may hold values from 0.1 to 1.9
- query_weight: bfloat16 [1536, 1024], P('seq'), may hold values from -4 to 4
- keyvalue_weight: bfloat16 [1536, 320], P('seq'), may hold values from -4 to 4
- output_weight: bfloat16 [1536, 1536], P(None, 'seq'), may hold values from -0.15625 to 0.15625
- rowcol_weight: bfloat16 [1536, 256], replicated, may hold values from -0.15625 to 0.15625
- pair_weight: bfloat16 [128, 128], replicated, may hold values from -0.5 to 0.5
Outputs:
- tokens: bfloat16 [2048, 1536], P(('grp', 'seq', 'col')), parts along dimension 0
- pair_out: bfloat16 [128, 64, 128], P(('grp', 'seq'), 'col'), parts along dimension 0
There are 2 independent parts, one for each index of `grp`. A program takes and returns all parts, laid end to end along the dimension named above; an argument that names none is the same for every part. Nothing has to cross between parts.
All inputs are finite; a program needn't handle non-finite values.
Results may differ from a plain program's by a relative error of at most 0.015.
Values may be sent and summed in bfloat16 or wider, within the bound.
A program may use at most 128 MiB of HBM per device.

v0:
```python
import jax
import jax.numpy as jnp
from jax import lax
from jax.sharding import PartitionSpec as P

DK = 128
DV = 192
POOL = 4
PAIR_POOL = 16


def with_halo(array, sides, width):
    for axis, dim in sides:
        size, length = (lax.axis_size(axis), array.shape[dim])
        up = [(i, (i + 1) % size) for i in range(size - 1)]
        down = [(j, i) for i, j in up]
        last = lax.slice_in_dim(array, length - width, length, axis=dim)
        first = lax.slice_in_dim(array, 0, width, axis=dim)
        before = lax.ppermute(last, axis, up)
        after = lax.ppermute(first, axis, down)
        array = jnp.concatenate([before, array, after], axis=dim)
    return array


def rms_scale(values, gain_vector):
    return (
        values * lax.rsqrt(jnp.mean(values * values, axis=-1, keepdims=True) + 1e-06) * gain_vector
    )


def attention_parts(queries, head_count):
    query_rows = queries.reshape(queries.shape[0] * head_count, DK)

    def absorb(running, pieces, first_row):
        running_max, running_sum, accumulated = running
        key_piece, value_piece = pieces
        scores = lax.dot_general(
            query_rows, key_piece, (((1,), (1,)), ((), ())), preferred_element_type=jnp.float32
        )
        newest_max = jnp.maximum(running_max, jnp.max(scores, axis=1))
        weights = jnp.exp(scores - newest_max[:, None])
        running_sum = jnp.sum(weights, axis=1)
        accumulated = jnp.dot(
            weights.astype(jnp.bfloat16), value_piece, preferred_element_type=jnp.float32
        )
        return (newest_max, running_sum, accumulated)

    row_count = query_rows.shape[0]
    initial = (
        jnp.full((row_count,), -1e30, jnp.float32),
        jnp.zeros((row_count,), jnp.float32),
        jnp.zeros((row_count, DV), jnp.float32),
    )
    return (absorb, initial)


def finish_attention(result, token_count):
    running_max, running_sum, accumulated = result
    return (accumulated / running_sum[:, None]).astype(jnp.bfloat16).reshape(token_count, -1)


def on_device(
    signal,
    conv_weight,
    conv_gain,
    embed_weight,
    attn_gain,
    query_weight,
    keyvalue_weight,
    output_weight,
    rowcol_weight,
    pair_weight,
):
    positions = signal.shape[0]
    tap_count = conv_weight.shape[0]
    halo_width = tap_count // 2
    padded = with_halo(signal, (("seq", 0),), halo_width)
    widened = lax.all_gather(padded, "col", axis=1, tiled=True)
    activated = jax.nn.gelu(
        rms_scale(widened.astype(jnp.float32), conv_gain), approximate=True
    ).astype(jnp.bfloat16)
    summed = signal.astype(jnp.float32)
    for tap_index in range(tap_count):
        summed = summed + jnp.dot(
            activated[tap_index : tap_index + positions],
            conv_weight[tap_index],
            preferred_element_type=jnp.float32,
        )
    pooled = jnp.mean(summed.reshape(positions // POOL, POOL, -1), axis=1).astype(jnp.bfloat16)
    embed_full = lax.all_gather(embed_weight, "seq", axis=1, tiled=True)
    col_count = lax.axis_size("col")
    embedded = lax.psum_scatter(
        jnp.dot(pooled, embed_full, preferred_element_type=jnp.float32).astype(jnp.bfloat16),
        "col",
        scatter_dimension=0,
        tiled=True,
    )
    normed = rms_scale(embedded.astype(jnp.float32), attn_gain).astype(jnp.bfloat16)
    head_count = query_weight.shape[1] // DK
    scaling = DK ** (-0.5)
    col_index = lax.axis_index("col")
    local_heads = head_count // col_count
    group_tokens = lax.all_gather(normed, "col", axis=0, tiled=True)
    group_count = group_tokens.shape[0]
    query_half = lax.dynamic_slice_in_dim(
        query_weight, col_index * local_heads * DK, local_heads * DK, 1
    )
    query_sum = jnp.dot(
        group_tokens,
        lax.all_gather(query_half, "seq", axis=0, tiled=True),
        preferred_element_type=jnp.float32,
    )
    keyvalue_sum = jnp.dot(
        group_tokens,
        lax.all_gather(keyvalue_weight, "seq", axis=0, tiled=True),
        preferred_element_type=jnp.float32,
    )
    queries = (query_sum * scaling).astype(jnp.bfloat16)
    keyvalue = keyvalue_sum.astype(jnp.bfloat16)
    absorb, initial = attention_parts(queries, local_heads)
    result = absorb(
        initial,
        (
            lax.all_gather(keyvalue[:, :DK], "seq", axis=0, tiled=True),
            lax.all_gather(keyvalue[:, DK:], "seq", axis=0, tiled=True),
        ),
        jnp.int32(0),
    )
    attended = finish_attention(result, group_count)
    output_half = lax.dynamic_slice_in_dim(
        output_weight, col_index * local_heads * DV, local_heads * DV, 0
    )
    partial_out = jnp.dot(
        attended,
        lax.all_gather(output_half, "seq", axis=1, tiled=True),
        preferred_element_type=jnp.float32,
    )
    attention_out = lax.psum_scatter(
        partial_out.astype(jnp.bfloat16), "col", scatter_dimension=0, tiled=True
    ).astype(jnp.float32)
    tokens = (embedded.astype(jnp.float32) + attention_out).astype(jnp.bfloat16)
    pair_pool = jnp.mean(
        tokens.astype(jnp.float32).reshape(-1, PAIR_POOL, tokens.shape[1]), axis=1
    ).astype(jnp.bfloat16)
    projected = jnp.dot(pair_pool, rowcol_weight, preferred_element_type=jnp.float32).astype(
        jnp.bfloat16
    )
    features = pair_weight.shape[0]
    row_block = lax.all_gather(projected, "col", axis=0, tiled=True)
    column_all = lax.all_gather(row_block[:, features:], "seq", axis=0, tiled=True)
    row_part = row_block[:, :features]
    column_span = column_all.shape[0] // col_count
    column_part = lax.dynamic_slice_in_dim(
        column_all, lax.axis_index("col") * column_span, column_span, 0
    )
    hidden = jax.nn.gelu(
        row_part.astype(jnp.float32)[:, None, :] + column_part.astype(jnp.float32)[None, :, :],
        approximate=True,
    ).astype(jnp.bfloat16)
    pair_out = jnp.dot(
        hidden.reshape(-1, features), pair_weight, preferred_element_type=jnp.float32
    ).astype(jnp.bfloat16)
    return (tokens, pair_out.reshape(row_part.shape[0], column_span, features))


def solution(mesh):
    placed = (
        P(("grp", "seq"), "col"),
        P(None, None, "col"),
        P(),
        P("col", "seq"),
        P(),
        P("seq", None),
        P("seq", None),
        P(None, "seq"),
        P(),
        P(),
    )
    return jax.shard_map(
        on_device,
        mesh=mesh,
        in_specs=placed,
        out_specs=(P(("grp", "seq", "col"), None), P(("grp", "seq"), "col", None)),
        check_vma=False,
    )
```

profile of v0, /device:TPU:0, one launch (start us, length us, event | category | flops | bytes accessed | tf_op | source)
XLA Modules:
  0.0 256.0 jit_solution(12248278608278916954)
XLA Ops:
  7.2 0.0 copy-start
  7.2 0.0 all-gather.13.cloned.1.call-start
  7.2 1.4 copy.19
  8.7 4.9 %collective-permute-start = (bf16[2,704]{1,0:T(2,128)(2,1)S(1)}, bf16[2,704]{1,0:T(2,128)(2,1)S(1)}, u32[]{:S(2)}, u32[]{:S(2)}) collective-permute-start(bf16[2,704]{1,0:T(2,128)(2,1)S(1)} %get-tuple-element.4), channel_id=1, source_target_pairs={{0,2},{2,4},{4,6},{6,8},{8,10},{10,12},{12,14},{1,3},{3,5},{5,7},{... | collective-permute-start | bytes 8456 | tf_op jit(solution)/shard_map/ppermute | solution.py:19
  13.6 1.3 collective-permute-start.1
  14.9 4.2 %collective-permute-done.1 = bf16[2,704]{1,0:T(2,128)(2,1)S(1)} collective-permute-done((bf16[2,704]{1,0:T(2,128)(2,1)S(1)}, bf16[2,704]{1,0:T(2,128)(2,1)S(1)}, u32[]{:S(2)}, u32[]{:S(2)}) %collective-permute-start.1) | collective-permute-done | bytes 2848 | tf_op jit(solution)/shard_map/ppermute | solution.py:20
  19.1 1.1 maximum_bitcast_fusion
  20.2 0.0 all-gather.13.cloned.1.call-update
  20.2 0.0 all-gather.7.cloned.1.call-start
  20.3 0.7 all-gather.7.cloned.1.call-update
  21.0 0.0 reduce-scatter.3.cloned.1.call-start
  21.0 10.3 %all-gather.13.cloned.1.call-done = bf16[2,704,516]{1,2,0:T(8,128)(2,1)} async-done(((bf16[1,704,516]{1,2,0:T(8,128)(2,1)}), bf16[2,704,516]{1,2,0:T(8,128)(2,1)}) %all-gather.13.cloned.1.call-update) | async-done | bytes 1453072 | tf_op jit(solution)/shard_map/all_gather | solution.py:78
  31.4 4.3 %copy.22 = f32[2,704,516]{1,0,2:T(2,128)} copy(bf16[2,704,516]{1,2,0:T(8,128)(2,1)} %all-gather.13.cloned.1.call-done) | data formatting | bytes 4359168 | tf_op jit(solution)/shard_map/convert_element_type | solution.py:80
  35.6 5.3 %reshape.62 = f32[1408,516]{0,1:T(8,128)} reshape(f32[2,704,516]{1,0,2:T(2,128)} %copy.22) | data formatting | bytes 5812224 | tf_op jit(solution)/shard_map/convert_element_type | solution.py:80
  41.0 2.4 multiply_reduce_fusion
  43.4 0.5 copy-done.1
  43.9 1.2 fusion.7
  45.1 0.0 copy-start.4
  45.1 3.0 %fusion.16 = f32[512,704]{0,1:T(8,128)S(1)} fusion(bf16[5,1408,704]{1,2,0:T(8,128)(2,1)} %param.11, bf16[516,1408]{1,0:T(8,128)(2,1)S(1)} %fusion.7), kind=kOutput, calls=%fused_computation.21 | convolution fusion | flops 1015021568 | bytes 4866048 | tf_op jit(solution)/shard_map/dot_general | solution.py:84
  48.1 1.4 copy-done.4
  49.6 1.3 fusion.12
  50.9 1.3 fusion.10
  52.2 0.0 copy-start.2
  52.2 1.3 fusion.8
  53.6 1.5 add_add_fusion
  55.1 1.6 copy.23
  56.7 1.8 reshape.50
  58.5 0.9 reduce_sum.46
  59.4 0.0 copy-start.5
  59.5 27.1 %all-gather.7.cloned.1.call-done = bf16[704,1536]{0,1:T(8,128)(2,1)} async-done(((bf16[704,192]{0,1:T(8,128)(2,1)}), bf16[704,1536]{0,1:T(8,128)(2,1)}) %all-gather.7.cloned.1.call-update) | async-done | bytes 2162704 | tf_op jit(solution)/shard_map/all_gather | solution.py:90
  86.6 3.3 %convolution_convert_fusion.1 = bf16[128,1536]{1,0:T(8,128)(2,1)} fusion(bf16[704,1536]{0,1:T(8,128)(2,1)} %all-gather.7.cloned.1.call-done, f32[128,704]{1,0:T(8,128)S(1)} %reduce_sum.46), kind=kOutput, calls=%fused_computation.11 | convolution fusion | flops 277200896 | bytes 2916352 | tf_op jit(solution)/shard_map/dot_general | solution.py:93
  89.9 0.0 reduce-scatter.3.cloned.1.call-update
  89.9 0.0 all-gather.9.cloned.1.call-start
  90.0 0.7 constant_dynamic-slice_fusion.1
  90.7 0.0 all-gather.9.cloned.1.call-update
  90.7 0.0 all-gather.11.cloned.1.call-start
  90.7 0.8 constant_dynamic-slice_fusion
  91.5 0.0 all-gather.11.cloned.1.call-update
  91.5 0.0 reduce-scatter.5.cloned.1.call-start
  91.6 34.7 %all_gather.34 = bf16[1536,320]{1,0:T(8,128)(2,1)S(1)} all-gather(bf16[192,320]{1,0:T(8,128)(2,1)S(1)} %copy-done.6), channel_id=1, replica_groups=mesh['grp'=2,'seq'=8,'col'=2] {'seq'}, dimensions={0}, use_global_device_ids=true | all-gather | bytes 1105920 | tf_op jit(solution)/shard_map/all_gather | solution.py:115
  126.3 1.1 fusion.39
  127.3 1.0 fusion.41
  128.4 2.3 all_gather.32
  130.7 0.5 convolution_convert_fusion.2
  131.2 17.2 %all-gather.9.cloned.1.call-done = bf16[1536,512]{1,0:T(8,128)(2,1)} async-done(((bf16[192,512]{1,0:T(8,128)(2,1)}), bf16[1536,512]{1,0:T(8,128)(2,1)}) %all-gather.9.cloned.1.call-update) | async-done | bytes 1572880 | tf_op jit(solution)/shard_map/all_gather | solution.py:110
  148.5 1.8 fusion.35
  150.3 0.1 reshape.51
  150.4 27.6 %all_gather.35 = bf16[1024,128]{0,1:T(8,128)(2,1)S(1)} all-gather(bf16[128,128]{0,1:T(8,128)(2,1)S(1)} %slice.71), channel_id=1, replica_groups=mesh['grp'=2,'seq'=8,'col'=2] {'seq'}, dimensions={0}, use_global_device_ids=true | all-gather | bytes 294912 | tf_op jit(solution)/shard_map/all_gather | solution.py:124
  177.9 29.5 %all_gather.36 = bf16[1024,192]{0,1:T(8,128)(2,1)S(1)} all-gather(bf16[128,192]{0,1:T(8,128)(2,1)S(1)} %slice.72), channel_id=1, replica_groups=mesh['grp'=2,'seq'=8,'col'=2] {'seq'}, dimensions={0}, use_global_device_ids=true | all-gather | bytes 442368 | tf_op jit(solution)/shard_map/all_gather | solution.py:125
  207.5 0.5 fusion.57
  208.0 0.5 fusion.23
  208.5 0.6 fusion.34
  209.1 0.1 copy.24
  209.2 0.3 reshape.52
  209.5 0.0 all-gather.11.cloned.1.call-done
  209.6 3.3 %convolution_convert_fusion = bf16[128,1536]{1,0:T(8,128)(2,1)} fusion(bf16[128,768]{1,0:T(8,128)(2,1)S(1)} %reshape.52, bf16[768,1536]{0,1:T(8,128)(2,1)} %all-gather.11.cloned.1.call-done), kind=kOutput, calls=%fused_computation.10 | convolution fusion | flops 302186496 | bytes 2949120 | tf_op jit(solution)/shard_map/dot_general | solution.py:133
  212.9 0.0 reduce-scatter.5.cloned.1.call-update
  212.9 5.2 %reduce-scatter.5.cloned.1.call-done = bf16[64,1536]{1,0:T(8,128)(2,1)} async-done(((bf16[128,1536]{1,0:T(8,128)(2,1)}), bf16[64,1536]{1,0:T(8,128)(2,1)}) %reduce-scatter.5.cloned.1.call-update) | async-done | bytes 196624 | tf_op jit(solution)/shard_map/reduce_scatter | solution.py:138
  218.1 1.7 convert_reduce_fusion
  219.8 0.2 fusion.36
  220.0 1.8 all-gather.1
  221.9 26.4 %all_gather.39 = bf16[64,128]{1,0:T(8,128)(2,1)S(1)} all-gather(bf16[8,128]{1,0:T(8,128)(2,1)S(1)} %get-tuple-element.7), channel_id=1, replica_groups=mesh['grp'=2,'seq'=8,'col'=2] {'seq'}, dimensions={0}, use_global_device_ids=true | all-gather | bytes 18432 | tf_op jit(solution)/shard_map/all_gather | solution.py:150
  248.3 0.1 fusion.51
  248.4 0.8 convolution_convert_fusion.3
  (28 shorter events, 0.1 us)
Async XLA Ops:
  7.2 212.6 %copy-start = (bf16[1536,256]{1,0:T(8,128)(2,1)S(1)}, bf16[1536,256]{1,0:T(8,128)(2,1)}, u32[]{:S(2)}) copy-start(bf16[1536,256]{1,0:T(8,128)(2,1)} %param.18) | copy-start | bytes 2359300
  7.2 24.2 %all-gather.13.cloned.1.call-start = ((), (), s32[]{:S(2)}) async-start(), calls=%async_computation.7 | async-start | bytes 2396160 | tf_op jit(solution)/shard_map/all_gather | solution.py:78
  8.7 6.2 %collective-permute-start = (bf16[2,704]{1,0:T(2,128)(2,1)S(1)}, bf16[2,704]{1,0:T(2,128)(2,1)S(1)}, u32[]{:S(2)}, u32[]{:S(2)}) collective-permute-start(bf16[2,704]{1,0:T(2,128)(2,1)S(1)} %get-tuple-element.4), channel_id=1, source_target_pairs={{0,2},{2,4},{4,6},{6,8},{8,10},{10,12},{12,14},{1,3},{3,5},{5,7},{... | collective-permute-start | bytes 8456 | tf_op jit(solution)/shard_map/ppermute | solution.py:19
  13.6 5.5 %collective-permute-start.1 = (bf16[2,704]{1,0:T(2,128)(2,1)S(1)}, bf16[2,704]{1,0:T(2,128)(2,1)S(1)}, u32[]{:S(2)}, u32[]{:S(2)}) collective-permute-start(bf16[2,704]{1,0:T(2,128)(2,1)S(1)} %get-tuple-element.5), channel_id=1, source_target_pairs={{2,0},{4,2},{6,4},{8,6},{10,8},{12,10},{14,12},{3,1},{5,3},{7,5},{... | collective-permute-start | bytes 8456 | tf_op jit(solution)/shard_map/ppermute | solution.py:20
  20.2 66.3 %all-gather.7.cloned.1.call-start = ((), (), s32[]{:S(2)}) async-start(), calls=%async_computation.2 | async-start | bytes 2654208 | tf_op jit(solution)/shard_map/all_gather | solution.py:90
  21.0 105.3 %reduce-scatter.3.cloned.1.call-start = ((), (), s32[]{:S(2)}) async-start(), calls=%async_computation.3 | async-start | bytes 589824 | tf_op jit(solution)/shard_map/reduce_scatter | solution.py:92
  41.0 2.9 %copy-start.1 = (f32[1408,516]{0,1:T(8,128)S(1)}, f32[1408,516]{0,1:T(8,128)}, u32[]{:S(2)}) copy-start(f32[1408,516]{0,1:T(8,128)} %reshape.62) | copy-start | bytes 8718340
  41.0 2.9 %copy-start.9 = (f32[1408]{0:T(1024)S(1)}, f32[1408]{0:T(1024)}, u32[]{:S(2)}) copy-start(f32[1408]{0:T(1024)} %param.12) | copy-start | bytes 16900
  45.1 4.4 %copy-start.4 = (bf16[5,1408,704]{1,2,0:T(8,128)(2,1)S(1)}, bf16[5,1408,704]{1,2,0:T(8,128)(2,1)}, u32[]{:S(2)}) copy-start(bf16[5,1408,704]{1,2,0:T(8,128)(2,1)} %param.11) | copy-start | bytes 29736964
  52.2 1.4 copy-start.2
  59.4 30.5 %copy-start.7 = (bf16[192,1024]{1,0:T(8,128)(2,1)S(1)}, bf16[192,1024]{1,0:T(8,128)(2,1)}, u32[]{:S(2)}) copy-start(bf16[192,1024]{1,0:T(8,128)(2,1)} %param.15) | copy-start | bytes 1179652
  59.4 31.3 %copy-start.5 = (bf16[1536,192]{0,1:T(8,128)(2,1)S(1)}, bf16[1536,192]{0,1:T(8,128)(2,1)}, u32[]{:S(2)}) copy-start(bf16[1536,192]{0,1:T(8,128)(2,1)} %param.17) | copy-start | bytes 1769476
  59.4 32.1 %copy-start.6 = (bf16[192,320]{1,0:T(8,128)(2,1)S(1)}, bf16[192,320]{1,0:T(8,128)(2,1)}, u32[]{:S(2)}) copy-start(bf16[192,320]{1,0:T(8,128)(2,1)} %param.16) | copy-start | bytes 368644
  89.9 37.5 %copy-start.10 = (f32[1536]{0:T(1024)S(1)}, f32[1536]{0:T(1024)}, u32[]{:S(2)}) copy-start(f32[1536]{0:T(1024)} %param.14) | copy-start | bytes 18436
  89.9 58.6 %all-gather.9.cloned.1.call-start = ((), (), s32[]{:S(2)}) async-start(), calls=%async_computation.4 | async-start | bytes 1769472 | tf_op jit(solution)/shard_map/all_gather | solution.py:110
  90.7 118.9 %all-gather.11.cloned.1.call-start = ((), (), s32[]{:S(2)}) async-start(), calls=%async_computation.5 | async-start | bytes 2654208 | tf_op jit(solution)/shard_map/all_gather | solution.py:135
  91.5 126.6 %reduce-scatter.5.cloned.1.call-start = ((), (), s32[]{:S(2)}) async-start(), calls=%async_computation.6 | async-start | bytes 589824 | tf_op jit(solution)/shard_map/reduce_scatter | solution.py:138
  209.2 8.9 %copy-start.3 = (bf16[64,1536]{1,0:T(8,128)(2,1)S(1)}, bf16[64,1536]{1,0:T(8,128)(2,1)}, u32[]{:S(2)}) copy-start(bf16[64,1536]{1,0:T(8,128)(2,1)} %reduce-scatter.3.cloned.1.call-done) | copy-start | bytes 589828
  209.5 38.8 %copy-start.8 = (bf16[128,128]{1,0:T(8,128)(2,1)S(1)}, bf16[128,128]{1,0:T(8,128)(2,1)}, u32[]{:S(2)}) copy-start(bf16[128,128]{1,0:T(8,128)(2,1)} %param.19) | copy-start | bytes 98308
Sparse Core Ops, SparseCore 0:
  20.3 10.9 all-gather.12
  33.5 52.9 all-gather.6
  90.0 6.3 reduce-scatter.2
  99.0 49.4 all-gather.8
  150.5 55.1 all-gather.10
  213.0 5.0 reduce-scatter.4
where the time goes:
time: 257 us; the launch traced here: 256 us
  blocking collectives  122 us (47%)
  waiting for transfers between devices  64.9 us (25%)
  matrix products  19.5 us (8%)
  local copies, waits for them, and re-layouts  18.4 us (7%)
  between operations  14.4 us (6%)
  other arithmetic  10.1 us (4%)
  starting transfers between devices  6.43 us (3%)
    all_gather x1, blocking collectives, on_device(): lax.all_gather(keyvalue_weight, 'seq', axis=0, tiled=True)  34.7 us
    all_gather x1, blocking collectives, on_device(): lax.all_gather(keyvalue[:, DK:], 'seq', axis=0, tiled=True)  29.5 us
    all_gather x1, blocking collectives, on_device(): lax.all_gather(keyvalue[:, :DK], 'seq', axis=0, tiled=True)  27.6 us
    all_gather x1, waiting for transfers between devices, on_device(): embed_full = lax.all_gather(embed_weight, 'seq', axis=1, tiled=True)  27.1 us
    all_gather x1, blocking collectives, on_device(): lax.all_gather(row_block[:, features:], 'seq', axis=0, tiled=True)  26.4 us
    all_gather x1, waiting for transfers between devices, on_device(): lax.all_gather(query_half, 'seq', axis=0, tiled=True)  17.2 us
    all_gather x1, waiting for transfers between devices, on_device(): widened = lax.all_gather(padded, 'col', axis=1, tiled=True)  10.3 us
    convert_element_type x2, local copies, waits for them, and re-layouts, on_device(): widened.astype(jnp.float32)  9.6 us
  transfers between devices with their start and end apart: 8, of which 5 were waited for; matrix products, arithmetic and copies ran while one was open for 13% of the time, Pallas kernels for 0%

commit v1 on v0

--- a/solution.py
+++ b/solution.py
@@ -1,6 +1,10 @@
+import functools
+
 import jax
 import jax.numpy as jnp
 from jax import lax
+from jax.experimental import pallas as pl
+from jax.experimental.pallas import tpu as pltpu
 from jax.sharding import PartitionSpec as P
 
 DK = 128
@@ -163,6 +167,491 @@
     return (tokens, pair_out.reshape(row_part.shape[0], column_span, features))
 
 
+EDGE = 16
+LEAD = 8
+Y = 2
+
+
+def fused_kernel(
+    taps,
+    heads,
+    signal,
+    conv_w,
+    conv_gain,
+    embed_w,
+    attn_gain,
+    query_w,
+    kv_w,
+    out_w,
+    rowcol,
+    pair_w,
+    tokens_out,
+    pair_out,
+    sig,
+    act,
+    halo,
+    conv_buf,
+    e_buf,
+    q_buf,
+    k_buf,
+    o_buf,
+    part,
+    other,
+    emb,
+    normed,
+    kv_all,
+    att,
+    cols,
+    hid,
+    loc_sem,
+    sig_sem,
+    w_sem,
+    p_sem,
+    kv_sem,
+    kp_sem,
+    ex_sem,
+    col_sem,
+):
+    f32, bf16 = jnp.float32, jnp.bfloat16
+    n = lax.axis_size("seq")
+    nz = n // Y
+    s = lax.axis_index("seq")
+    c = lax.axis_index("col")
+    x = lax.axis_index("grp")
+    z, y = s // Y, s % Y
+    half = sig.shape[2]
+    positions = sig.shape[1]
+    count = positions // POOL
+    width = e_buf.shape[2]
+    halo_width = taps // 2
+    started = []
+
+    def remote(src, dst, sems, index, to):
+        copy = pltpu.make_async_remote_copy(
+            src_ref=src,
+            dst_ref=dst,
+            send_sem=sems.at[(0,) + index],
+            recv_sem=sems.at[(1,) + index],
+            device_id=to,
+            device_id_type=pl.DeviceIdType.MESH,
+        )
+        copy.start()
+        started.append(copy)
+        return copy
+
+    def seq_of(z_index, y_index):
+        return z_index * Y + y_index
+
+    def z_from(dz):
+        return (z + nz - dz) % nz
+
+    def z_to(dz):
+        return (z + dz) % nz
+
+    partner = {"col": 1 - c}
+    y_peer = {"seq": seq_of(z, 1 - y)}
+    x_peer = {"grp": 1 - x}
+
+    local = [pltpu.make_async_copy(signal, sig.at[0], loc_sem.at[0])]
+    local[0].start()
+    k_rows = kv_w.shape[0] // 2
+    q_cols = query_w.shape[1] // 2
+    o_rows = out_w.shape[0] // 2
+    kv_own = kv_w.at[pl.ds(pl.multiple_of(c * k_rows, 16), k_rows)]
+    q_own = query_w.at[:, pl.ds(pl.multiple_of(c * q_cols, 128), q_cols)]
+    o_own = out_w.at[pl.ds(pl.multiple_of(c * o_rows, 16), o_rows)]
+
+    def e_at(owner):
+        return e_buf.at[owner]
+
+    def q_at(owner):
+        return q_buf.at[owner]
+
+    def k_at(owner, core=None):
+        core = c if core is None else core
+        return k_buf.at[owner, pl.ds(pl.multiple_of(core * k_rows, 16), k_rows)]
+
+    def o_at(owner):
+        return o_buf.at[owner]
+
+    pieces = [(embed_w, e_at), (kv_own, k_at), (q_own, q_at), (o_own, o_at)]
+    E, KV, Q, O = range(4)
+    for t in range(taps):
+        local.append(pltpu.make_async_copy(conv_w.at[t], conv_buf.at[t], loc_sem.at[1 + t]))
+    for w, (own, at) in enumerate(pieces):
+        local.append(pltpu.make_async_copy(own, at(s), loc_sem.at[1 + taps + w]))
+    for copy in local[1:]:
+        copy.start()
+
+    barrier = pltpu.get_barrier_semaphore()
+    for d in range(n):
+        for e in range(2):
+            if d or e:
+                pl.semaphore_signal(
+                    barrier,
+                    inc=1,
+                    device_id={"seq": (s + d) % n, "col": (c + e) % 2},
+                    device_id_type=pl.DeviceIdType.MESH,
+                )
+    pl.semaphore_signal(barrier, inc=1, device_id=x_peer, device_id_type=pl.DeviceIdType.MESH)
+    pl.semaphore_wait(barrier, 2 * n)
+
+    signal_copies = [remote(signal, sig.at[1], sig_sem, (0,), partner)]
+    last = signal.at[pl.ds(positions - EDGE, EDGE)]
+    first = signal.at[pl.ds(0, EDGE)]
+    for e in range(2):
+        core = (c + e) % 2
+        up = {"seq": (s + 1) % n, "col": core}
+        down = {"seq": (s + n - 1) % n, "col": core}
+        signal_copies.append(remote(last, halo.at[e, 0], sig_sem, (1 + 2 * e,), up))
+        signal_copies.append(remote(first, halo.at[e, 1], sig_sem, (2 + 2 * e,), down))
+
+    def rows_half(ref, h):
+        rows = ref.shape[0] // 2
+        return ref.at[pl.ds(pl.multiple_of(h * rows, 16), rows)]
+
+    copies = {}
+
+    def send(w, key, slot, src, dst, to):
+        copies[w, key] = remote(src, dst, w_sem, (w, slot), to)
+
+    def along_z(w):
+        own, at = pieces[w]
+        for dz in range(1, nz):
+            to = {"seq": seq_of(z_to(dz), y)}
+            send(w, ("z", dz), dz, rows_half(own, x), rows_half(at(s), x), to)
+
+    def own_y(w):
+        own, at = pieces[w]
+        send(w, ("y", 0), 0, own, at(s), y_peer)
+
+    def stage2(w):
+        _, at = pieces[w]
+        for dz in range(1, nz):
+            copies[w, ("z", dz)].wait_recv()
+            ref = rows_half(at(seq_of(z_from(dz), y)), x)
+            send(w, ("y", dz), nz + dz, ref, ref, y_peer)
+            send(w, ("x", dz), 2 * nz + dz, ref, ref, x_peer)
+
+    def stage3(w):
+        _, at = pieces[w]
+        for dz in range(1, nz):
+            copies[w, ("y", dz)].wait_recv()
+            ref = rows_half(at(seq_of(z_from(dz), 1 - y)), x)
+            send(w, ("xy", dz), 3 * nz + dz, ref, ref, x_peer)
+
+    def owners():
+        order = [(0, True), (0, False)]
+        for dz in range(1, nz):
+            order += [(dz, True), (dz, False)]
+        return order
+
+    def owner_of(dz, same):
+        return seq_of(z_from(dz), y if same else 1 - y)
+
+    def arrived(w, dz, same):
+        if dz == 0:
+            if same:
+                local[1 + taps + w].wait()
+            else:
+                copies[w, ("y", 0)].wait_recv()
+        else:
+            copies[w, ("x" if same else "xy", dz)].wait_recv()
+
+    along_z(E)
+    own_y(E)
+    along_z(KV)
+    along_z(Q)
+    along_z(O)
+
+    for copy in signal_copies:
+        copy.wait_recv()
+    local[0].wait()
+    inside = [s > 0, s < n - 1]
+
+    def squares(v):
+        return jnp.sum(v * v, axis=1, keepdims=True)
+
+    channels = 2 * half
+    gains = [conv_gain[pl.ds(c, 1), :], conv_gain[pl.ds(1 - c, 1), :]]
+
+    def activate(v, scale, gain):
+        return jax.nn.gelu(v * scale * gain, approximate=True)
+
+    block = 64
+    lanes = act.shape[3]
+    tiles = [(q, min(lanes, half - q * lanes)) for q in range(act.shape[1])]
+
+    def put_rows(h, rows, v):
+        for q, size in tiles:
+            act[h, q, rows, :size] = v[:, q * lanes : q * lanes + size]
+
+    def pooled_rows(h, begin):
+        out = []
+        for q, size in tiles:
+            v = act[h, q, pl.ds(begin, count, stride=POOL), :]
+            for j in range(1, POOL):
+                v = v + act[h, q, pl.ds(begin + j, count, stride=POOL), :]
+            out.append((v * (1.0 / POOL))[:, :size])
+        return jnp.concatenate(out, axis=1)
+
+    @pl.loop(0, positions // block)
+    def _(i):
+        rows = pl.ds(pl.multiple_of(i * block, block), block)
+        put = pl.ds(pl.multiple_of(LEAD + i * block, 8), block)
+        a, b = sig[0, rows, :].astype(f32), sig[1, rows, :].astype(f32)
+        scale = lax.rsqrt((squares(a) + squares(b)) * (1.0 / channels) + 1e-06)
+        put_rows(0, put, activate(a, scale, gains[0]))
+        put_rows(1, put, activate(b, scale, gains[1]))
+
+    for side in range(2):
+        a, b = halo[0, side].astype(f32), halo[1, side].astype(f32)
+        scale = lax.rsqrt((squares(a) + squares(b)) * (1.0 / channels) + 1e-06)
+        for h, v in enumerate((a, b)):
+            v = jnp.where(inside[side], activate(v, scale, gains[h]), 0.0)
+            if side == 0:
+                put_rows(h, pl.ds(0, LEAD), v[EDGE - LEAD :])
+            else:
+                put_rows(h, pl.ds(LEAD + positions, LEAD), v[:LEAD])
+
+    stage2(E)
+
+    total = jnp.zeros((count, half), f32)
+    for t in range(taps):
+        local[1 + t].wait()
+        for h in range(2):
+            window = pooled_rows(h, LEAD + t - halo_width).astype(bf16)
+            core = c if h == 0 else 1 - c
+            rows = pl.ds(pl.multiple_of(core * half, 16), half)
+            total = total + jnp.dot(window, conv_buf[t, rows, :], preferred_element_type=f32)
+
+    @pl.loop(0, positions // block)
+    def _(i):
+        rows = pl.ds(pl.multiple_of(i * block, block), block)
+        put = pl.ds(pl.multiple_of(LEAD + i * block, 8), block)
+        put_rows(0, put, sig[0, rows, :].astype(f32))
+
+    pooled = (total + pooled_rows(0, LEAD)).astype(bf16)
+
+    stage3(E)
+    own_y(KV)
+    own_y(Q)
+
+    swaps = []
+    for k, (dz, same) in enumerate(owners()):
+        owner = owner_of(dz, same)
+        arrived(E, dz, same)
+        part[0, owner] = jnp.dot(pooled, e_buf[owner], preferred_element_type=f32).astype(bf16)
+        swaps.append(remote(part.at[0, owner], other.at[0, owner], ex_sem, (0, k), partner))
+    stage2(KV)
+    stage2(Q)
+    for copy in swaps:
+        copy.wait_recv()
+    square = jnp.zeros((count, 1), f32)
+    for b in range(n):
+        v = (part[0, b].astype(f32) + other[0, b].astype(f32)).astype(bf16)
+        emb[b] = v
+        square = square + squares(v.astype(f32))
+    scale = lax.rsqrt(square * (1.0 / (n * width)) + 1e-06)
+    for b in range(n):
+        normed[b] = (emb[b].astype(f32) * scale * attn_gain[pl.ds(b, 1), :]).astype(bf16)
+
+    stage3(KV)
+    stage3(Q)
+    own_y(O)
+
+    passed = []
+    for k, (dz, same) in enumerate(owners()):
+        arrived(KV, dz, same)
+        ref = k_at(owner_of(dz, same))
+        passed.append(remote(ref, ref, p_sem, (k,), partner))
+    for copy in passed:
+        copy.wait_recv()
+    own_tokens = pl.ds(pl.multiple_of(c * (count // 2), 16), count // 2)
+    kv = jnp.zeros((count // 2, k_buf.shape[2]), f32)
+    for b in range(n):
+        kv = kv + jnp.dot(normed[b, own_tokens, :], k_buf[b], preferred_element_type=f32)
+
+    def kv_at(owner):
+        return kv_all.at[owner, own_tokens]
+
+    kv_all[s, own_tokens, :] = kv.astype(bf16)
+    mine = kv_at(s)
+    kv_copies = {}
+    for dz in range(1, nz):
+        to = {"seq": seq_of(z_to(dz), y)}
+        kv_copies["z", dz] = remote(mine, mine, kv_sem, (dz,), to)
+    kv_copies["y", 0] = remote(mine, mine, kv_sem, (0,), y_peer)
+    across = [remote(mine, mine, kp_sem, (0,), partner)]
+
+    queries = jnp.zeros((count, q_cols), f32)
+    for dz, same in owners():
+        arrived(Q, dz, same)
+    for b in range(n):
+        queries = queries + jnp.dot(normed[b], q_buf[b], preferred_element_type=f32)
+    queries = (queries * (DK**-0.5)).astype(bf16)
+
+    for dz in range(1, nz):
+        kv_copies["z", dz].wait_recv()
+        ref = kv_at(seq_of(z_from(dz), y))
+        kv_copies["y", dz] = remote(ref, ref, kv_sem, (nz + dz,), y_peer)
+        across.append(remote(ref, ref, kp_sem, (dz,), partner))
+    stage2(O)
+    for dz in range(nz):
+        kv_copies["y", dz].wait_recv()
+        ref = kv_at(seq_of(z_from(dz), 1 - y))
+        across.append(remote(ref, ref, kp_sem, (nz + dz,), partner))
+    for copy in across:
+        copy.wait_recv()
+
+    everything = kv_all[...].reshape(n * count, kv_all.shape[2])
+    keys, values = everything[:, :DK], everything[:, DK:]
+    for h in range(heads):
+        scores = lax.dot_general(
+            queries[:, h * DK : (h + 1) * DK],
+            keys,
+            (((1,), (1,)), ((), ())),
+            preferred_element_type=f32,
+        )
+        weights = jnp.exp(scores - jnp.max(scores, axis=1, keepdims=True))
+        norm = jnp.sum(weights, axis=1, keepdims=True)
+        mixed = jnp.dot(weights.astype(bf16), values, preferred_element_type=f32)
+        att[h] = (mixed / norm).astype(bf16)
+
+    stage3(O)
+    swaps = []
+    for k, (dz, same) in enumerate(owners()):
+        owner = owner_of(dz, same)
+        arrived(O, dz, same)
+        acc = jnp.zeros((count, width), f32)
+        for h in range(heads):
+            acc = acc + jnp.dot(
+                att[h], o_buf[owner, h * DV : (h + 1) * DV, :], preferred_element_type=f32
+            )
+        part[1, owner] = acc.astype(bf16)
+        swaps.append(remote(part.at[1, owner], other.at[1, owner], ex_sem, (1, k), partner))
+    for copy in swaps:
+        copy.wait_recv()
+
+    rows_n = count // PAIR_POOL
+    row_of = lax.broadcasted_iota(jnp.int32, (rows_n, count), 0)
+    token_of = lax.broadcasted_iota(jnp.int32, (rows_n, count), 1) // PAIR_POOL
+    pool = jnp.where(row_of == token_of, 1.0 / PAIR_POOL, 0.0).astype(bf16)
+    features = pair_w.shape[0]
+    projected = jnp.zeros((rows_n, 2 * features), f32)
+    for b in range(n):
+        v = emb[b].astype(f32) + (part[1, b].astype(f32) + other[1, b].astype(f32))
+        emb[b] = v.astype(bf16)
+        pair_pool = jnp.dot(pool, emb[b], preferred_element_type=f32).astype(bf16)
+        projected = projected + jnp.dot(pair_pool, rowcol[b], preferred_element_type=f32)
+    projected = projected.astype(bf16).astype(f32)
+    cols[s] = projected[:, features:]
+    col_copies = []
+    for d in range(1, n):
+        to = {"seq": (s + d) % n}
+        col_copies.append(remote(cols.at[s], cols.at[s], col_sem, (d,), to))
+    for b in range(n):
+        tokens_out[b] = emb[b, own_tokens, :]
+    for copy in col_copies:
+        copy.wait_recv()
+    row_part = projected[:, None, :features]
+    for j in range(n // 2):
+        column = cols[c * (n // 2) + j]
+        hid[:, pl.ds(j * rows_n, rows_n), :] = jax.nn.gelu(
+            row_part + column[None, :, :], approximate=True
+        )
+    hidden = hid[...].reshape(rows_n * (n // 2) * rows_n, features).astype(bf16)
+    result = jnp.dot(hidden, pair_w[...], preferred_element_type=f32)
+    pair_out[...] = result.reshape(pair_out.shape).astype(bf16)
+    for copy in started:
+        copy.wait_send()
+
+
+def on_device_fused(
+    signal,
+    conv_weight,
+    conv_gain,
+    embed_weight,
+    attn_gain,
+    query_weight,
+    keyvalue_weight,
+    output_weight,
+    rowcol_weight,
+    pair_weight,
+):
+    bf16, f32 = jnp.bfloat16, jnp.float32
+    n = lax.axis_size("seq")
+    nz = n // Y
+    positions, half = signal.shape
+    taps, channels, _ = conv_weight.shape
+    count = positions // POOL
+    width = embed_weight.shape[1]
+    q_cols = query_weight.shape[1] // 2
+    heads = q_cols // DK
+    kv_cols = keyvalue_weight.shape[1]
+    rows_n = count // PAIR_POOL
+    features = pair_weight.shape[0]
+    any_spec = pl.BlockSpec(memory_space=pl.ANY)
+    vmem = pl.BlockSpec(memory_space=pltpu.VMEM)
+    dma = pltpu.SemaphoreType.DMA
+    tokens, pair = pl.pallas_call(
+        functools.partial(fused_kernel, taps, heads),
+        out_shape=(
+            jax.ShapeDtypeStruct((n, count // 2, width), bf16),
+            jax.ShapeDtypeStruct((rows_n, rows_n * n // 2, features), bf16),
+        ),
+        in_specs=[any_spec, any_spec, vmem, any_spec, vmem]
+        + [any_spec, any_spec, any_spec, vmem, vmem],
+        out_specs=(vmem, vmem),
+        scratch_shapes=[
+            pltpu.VMEM((2, positions, half), bf16),
+            pltpu.VMEM((2, pl.cdiv(half, 128), positions + 2 * LEAD, 128), f32),
+            pltpu.VMEM((2, 2, EDGE, half), bf16),
+            pltpu.VMEM((taps, channels, half), bf16),
+            pltpu.VMEM((n, half, width), bf16),
+            pltpu.VMEM((n, width, q_cols), bf16),
+            pltpu.VMEM((n, width, kv_cols), bf16),
+            pltpu.VMEM((n, heads * DV, width), bf16),
+            pltpu.VMEM((2, n, count, width), bf16),
+            pltpu.VMEM((2, n, count, width), bf16),
+            pltpu.VMEM((n, count, width), bf16),
+            pltpu.VMEM((n, count, width), bf16),
+            pltpu.VMEM((n, count, kv_cols), bf16),
+            pltpu.VMEM((heads, count, DV), bf16),
+            pltpu.VMEM((n, rows_n, features), f32),
+            pltpu.VMEM((rows_n, rows_n * n // 2, features), f32),
+            dma((5 + taps,)),
+            dma((2, 5)),
+            dma((2, 4, 4 * nz)),
+            dma((2, n)),
+            dma((2, n)),
+            dma((2, n)),
+            dma((2, 2, n)),
+            dma((2, n)),
+        ],
+        compiler_params=pltpu.CompilerParams(
+            collective_id=0, has_side_effects=True, vmem_limit_bytes=60 * 1024 * 1024
+        ),
+    )(
+        signal,
+        conv_weight,
+        conv_gain.reshape(2, half),
+        embed_weight,
+        attn_gain.reshape(n, width),
+        query_weight,
+        keyvalue_weight,
+        output_weight,
+        rowcol_weight.reshape(n, width, 2 * features),
+        pair_weight,
+    )
+    return jnp.transpose(tokens, (1, 0, 2)).reshape(count // 2, n * width), pair
+
+
+def fits(mesh):
+    n = mesh.shape["seq"]
+    return n == 8 and mesh.shape["col"] == 2 and mesh.shape["grp"] == 2
+
+
 def solution(mesh):
     placed = (
         P(("grp", "seq"), "col"),
@@ -177,7 +666,7 @@
         P(),
     )
     return jax.shard_map(
-        on_device,
+        on_device_fused if fits(mesh) else on_device,
         mesh=mesh,
         in_specs=placed,
         out_specs=(P(("grp", "seq", "col"), None), P(("grp", "seq"), "col", None)),

time: 257 us -> 141 us (0.55)
  blocking collectives: 122 us -> 0 us
  Pallas kernels: 0 us -> 112 us
  waiting for transfers between devices: 64.9 us -> 0 us
  matrix products: 19.5 us -> 0 us
  between operations: 14.4 us -> 0.64 us
  other arithmetic: 10.1 us -> 0 us
  local copies, waits for them, and re-layouts: 18.4 us -> 26.8 us
  starting transfers between devices: 6.43 us -> 0 us
    all_gather x6 -> x0, blocking collectives: 122 us -> none  [the longest x1 34.7 us: on_device(): lax.all_gather(keyvalue_weight, 'seq', axis=0, tiled=True)]
    pallas_call x0 -> x1, Pallas kernels: none -> 112 us  [on_device_fused(): pl.pallas_call(functools.partial(fused_kernel, taps, heads), out_shape=(j...]
    all_gather x4 -> x0, waiting for transfers between devices: 54.7 us -> none  [the longest x1 27.1 us: on_device(): embed_full = lax.all_gather(embed_weight, 'seq', axis=1, tiled=True)]
    dot_general x13 -> x0, matrix products: 19.5 us -> none  [the longest x5 8.49 us: on_device(): jnp.dot(activated[tap_index:tap_index + positions], conv_weight[tap_index...]
    unnamed x24 -> x5, local copies, waits for them, and re-layouts: 3.45 us -> 22 us
    convert_element_type x3 -> x0, local copies, waits for them, and re-layouts: 9.74 us -> none  [the longest x2 9.6 us: on_device(): widened.astype(jnp.float32)]
    reduce_sum x5 -> x0, other arithmetic: 6.57 us -> none  [the longest x2 3.46 us: rms_scale(): jnp.mean(values * values, axis=-1, keepdims=True) + 1e-06]
    ppermute x2 -> x0, starting transfers between devices: 6.19 us -> none  [the longest x1 4.9 us: with_halo(): before = lax.ppermute(last, axis, up)]
  transfers between devices with their start and end apart: 8 -> 0, of which waited for: 5 -> 0; matrix products, arithmetic and copies ran while one was open for 13% -> 0% of each run, Pallas kernels for 0% -> 0%
where the time goes in v1:
time: 141 us; the launch traced here: 140 us
  Pallas kernels  112 us (79%)
  local copies, waits for them, and re-layouts  26.8 us (19%)
    pallas_call x1, Pallas kernels, on_device_fused(): pl.pallas_call(functools.partial(fused_kernel, taps, heads), out_shape=(j...  112 us
    unnamed x5, local copies, waits for them, and re-layouts  22 us

profile of v1, /device:TPU:0, one launch (start us, length us, event | category | flops | bytes accessed | tf_op | source)
XLA Modules:
  0.0 139.9 jit_solution(6052289326213590774)
XLA Ops:
  0.6 1.4 reshape.16.conv_gain
  2.0 1.4 reshape.17.attn_gain
  3.4 1.9 %copy.18.embed_w = bf16[704,192]{1,0:T(8,128)(2,1)} copy(bf16[704,192]{0,1:T(8,128)(2,1)} %param.13) | data formatting | bytes 540672 | tf_op args[3]
  5.2 2.3 %copy.16.signal = bf16[512,704]{1,0:T(8,128)(2,1)} copy(bf16[512,704]{0,1:T(8,128)(2,1)} %param.10) | data formatting | bytes 1441792 | tf_op args[0]
  7.5 2.2 %copy.19.out_w = bf16[1536,192]{1,0:T(8,128)(2,1)} copy(bf16[1536,192]{0,1:T(8,128)(2,1)} %param.17) | data formatting | bytes 1179648 | tf_op args[7]
  9.7 14.2 %copy.17.conv_w = bf16[5,1408,704]{2,1,0:T(8,128)(2,1)} copy(bf16[5,1408,704]{1,2,0:T(8,128)(2,1)} %param.11) | data formatting | bytes 19824640 | tf_op args[1]
  23.9 112.5 %shard_map.113 = (bf16[8,64,192]{2,1,0:T(8,128)(2,1)}, bf16[8,32,128]{2,1,0:T(8,128)(2,1)}) custom-call(bf16[512,704]{1,0:T(8,128)(2,1)} %copy.16.signal, bf16[5,1408,704]{2,1,0:T(8,128)(2,1)} %copy.17.conv_w, f32[2,704]{1,0:T(2,128)} %reshape.16.conv_gain, bf16[704,192]{1,0:T(8,128)(2,1)} %copy.18.embed_w, f32[8,192]{1,0:T(8,128)} %reshape.17.attn_gain, ...), custom_call_target="tpu_custom_call" | custom-call | tf_op jit(solution)/shard_map/pallas_call | solution.py:597
  136.4 1.1 copy.20
  137.5 0.9 reshape.19
  138.4 1.5 %copy.22 = bf16[8,32,128]{2,1,0:T(8,128)(2,1)} copy(bf16[8,32,128]{2,1,0:T(8,128)(2,1)} %get-tuple-element.9) | data formatting | bytes 131072

commit v2 on v1

--- a/solution.py
+++ b/solution.py
@@ -168,7 +168,6 @@
 
 
 EDGE = 16
-LEAD = 8
 Y = 2
 
 
@@ -189,6 +188,8 @@
     pair_out,
     sig,
     act,
+    win,
+    edge,
     halo,
     conv_buf,
     e_buf,
@@ -200,7 +201,6 @@
     emb,
     normed,
     kv_all,
-    att,
     cols,
     hid,
     loc_sem,
@@ -219,10 +219,10 @@
     c = lax.axis_index("col")
     x = lax.axis_index("grp")
     z, y = s // Y, s % Y
-    half = sig.shape[2]
-    positions = sig.shape[1]
+    half = sig.shape[1]
+    positions = sig.shape[2]
     count = positions // POOL
-    width = e_buf.shape[2]
+    width = e_buf.shape[1]
     halo_width = taps // 2
     started = []
 
@@ -256,10 +256,10 @@
     local[0].start()
     k_rows = kv_w.shape[0] // 2
     q_cols = query_w.shape[1] // 2
-    o_rows = out_w.shape[0] // 2
+    o_cols = out_w.shape[1] // 2
     kv_own = kv_w.at[pl.ds(pl.multiple_of(c * k_rows, 16), k_rows)]
     q_own = query_w.at[:, pl.ds(pl.multiple_of(c * q_cols, 128), q_cols)]
-    o_own = out_w.at[pl.ds(pl.multiple_of(c * o_rows, 16), o_rows)]
+    o_own = out_w.at[:, pl.ds(pl.multiple_of(c * o_cols, 128), o_cols)]
 
     def e_at(owner):
         return e_buf.at[owner]
@@ -276,6 +276,7 @@
 
     pieces = [(embed_w, e_at), (kv_own, k_at), (q_own, q_at), (o_own, o_at)]
     E, KV, Q, O = range(4)
+    whole = (O,)
     for t in range(taps):
         local.append(pltpu.make_async_copy(conv_w.at[t], conv_buf.at[t], loc_sem.at[1 + t]))
     for w, (own, at) in enumerate(pieces):
@@ -297,14 +298,6 @@
     pl.semaphore_wait(barrier, 2 * n)
 
     signal_copies = [remote(signal, sig.at[1], sig_sem, (0,), partner)]
-    last = signal.at[pl.ds(positions - EDGE, EDGE)]
-    first = signal.at[pl.ds(0, EDGE)]
-    for e in range(2):
-        core = (c + e) % 2
-        up = {"seq": (s + 1) % n, "col": core}
-        down = {"seq": (s + n - 1) % n, "col": core}
-        signal_copies.append(remote(last, halo.at[e, 0], sig_sem, (1 + 2 * e,), up))
-        signal_copies.append(remote(first, halo.at[e, 1], sig_sem, (2 + 2 * e,), down))
 
     def rows_half(ref, h):
         rows = ref.shape[0] // 2
@@ -319,7 +312,10 @@
         own, at = pieces[w]
         for dz in range(1, nz):
             to = {"seq": seq_of(z_to(dz), y)}
-            send(w, ("z", dz), dz, rows_half(own, x), rows_half(at(s), x), to)
+            if w in whole:
+                send(w, ("z", dz), dz, own, at(s), to)
+            else:
+                send(w, ("z", dz), dz, rows_half(own, x), rows_half(at(s), x), to)
 
     def own_y(w):
         own, at = pieces[w]
@@ -331,7 +327,8 @@
             copies[w, ("z", dz)].wait_recv()
             ref = rows_half(at(seq_of(z_from(dz), y)), x)
             send(w, ("y", dz), nz + dz, ref, ref, y_peer)
-            send(w, ("x", dz), 2 * nz + dz, ref, ref, x_peer)
+            if w not in whole:
+                send(w, ("x", dz), 2 * nz + dz, ref, ref, x_peer)
 
     def stage3(w):
         _, at = pieces[w]
@@ -355,8 +352,10 @@
                 local[1 + taps + w].wait()
             else:
                 copies[w, ("y", 0)].wait_recv()
-        else:
-            copies[w, ("x" if same else "xy", dz)].wait_recv()
+        elif not same:
+            copies[w, ("xy", dz)].wait_recv()
+        elif w not in whole:
+            copies[w, ("x", dz)].wait_recv()
 
     along_z(E)
     own_y(E)
@@ -364,101 +363,109 @@
     along_z(Q)
     along_z(O)
 
+    row = lax.broadcasted_iota(jnp.int32, (EDGE, positions), 0)
+    place = lax.broadcasted_iota(jnp.int32, (EDGE, positions), 1)
+    wanted = jnp.where(row < EDGE // 2, row, row - EDGE // 2 + positions - halo_width)
+    in_use = lax.rem(row, EDGE // 2) < halo_width
+    pick = jnp.where((place == wanted) & in_use, 1.0, 0.0).astype(bf16)
+    local[0].wait()
+    over_rows = (((1,), (1,)), ((), ()))
+    edge[...] = lax.dot_general(pick, sig[0], over_rows, preferred_element_type=f32).astype(bf16)
+    for e in range(2):
+        core = (c + e) % 2
+        up = {"seq": (s + 1) % n, "col": core}
+        down = {"seq": (s + n - 1) % n, "col": core}
+        signal_copies.append(remote(edge, halo.at[e, 0], sig_sem, (1 + 2 * e,), up))
+        signal_copies.append(remote(edge, halo.at[e, 1], sig_sem, (2 + 2 * e,), down))
+
+    def windows(position):
+        column = lax.broadcasted_iota(jnp.int32, position.shape, 1)
+        tap = column // count
+        begin = (column - tap * count) * POOL + tap - halo_width
+        hit = (position >= begin) & (position < begin + POOL)
+        return jnp.where(hit, 1.0 / POOL, 0.0).astype(bf16)
+
+    mean_of = windows(lax.broadcasted_iota(jnp.int32, (positions, taps * count), 0))
+    edge_row = lax.broadcasted_iota(jnp.int32, (EDGE, taps * count), 0)
+    edge_means = [windows(edge_row - EDGE // 2 - halo_width), windows(edge_row + positions)]
+    edge_means = [
+        jnp.where((edge_row >= EDGE // 2) & (s > 0), edge_means[0], 0.0).astype(bf16),
+        jnp.where((edge_row < EDGE // 2) & (s < n - 1), edge_means[1], 0.0).astype(bf16),
+    ]
+    channels = 2 * half
+    gains = [conv_gain[pl.ds(c, 1), :], conv_gain[pl.ds(1 - c, 1), :]]
+    gain_columns = [jnp.broadcast_to(g, (128, half)).T for g in gains]
+
     for copy in signal_copies:
         copy.wait_recv()
-    local[0].wait()
-    inside = [s > 0, s < n - 1]
-
-    def squares(v):
-        return jnp.sum(v * v, axis=1, keepdims=True)
-
-    channels = 2 * half
-    gains = [conv_gain[pl.ds(c, 1), :], conv_gain[pl.ds(1 - c, 1), :]]
-
-    def activate(v, scale, gain):
-        return jax.nn.gelu(v * scale * gain, approximate=True)
 
     block = 64
-    lanes = act.shape[3]
-    tiles = [(q, min(lanes, half - q * lanes)) for q in range(act.shape[1])]
-
-    def put_rows(h, rows, v):
-        for q, size in tiles:
-            act[h, q, rows, :size] = v[:, q * lanes : q * lanes + size]
-
-    def pooled_rows(h, begin):
-        out = []
-        for q, size in tiles:
-            v = act[h, q, pl.ds(begin, count, stride=POOL), :]
-            for j in range(1, POOL):
-                v = v + act[h, q, pl.ds(begin + j, count, stride=POOL), :]
-            out.append((v * (1.0 / POOL))[:, :size])
-        return jnp.concatenate(out, axis=1)
-
-    @pl.loop(0, positions // block)
-    def _(i):
-        rows = pl.ds(pl.multiple_of(i * block, block), block)
-        put = pl.ds(pl.multiple_of(LEAD + i * block, 8), block)
-        a, b = sig[0, rows, :].astype(f32), sig[1, rows, :].astype(f32)
-        scale = lax.rsqrt((squares(a) + squares(b)) * (1.0 / channels) + 1e-06)
-        put_rows(0, put, activate(a, scale, gains[0]))
-        put_rows(1, put, activate(b, scale, gains[1]))
-
+    square = jnp.zeros((1, positions), f32)
+    for h in range(2):
+        v = sig[h].astype(f32)
+        square = square + jnp.sum(v * v, axis=0, keepdims=True)
+    scale = lax.rsqrt(square * (1.0 / channels) + 1e-06)
+    for h in range(2):
+        for i in range(half // block):
+            rows = slice(i * block, (i + 1) * block)
+            v = sig[h, rows, :].astype(f32) * scale * gain_columns[h][rows, :1]
+            act[h, rows, :] = jax.nn.gelu(v, approximate=True).astype(bf16)
+
+    edges = [[], []]
     for side in range(2):
         a, b = halo[0, side].astype(f32), halo[1, side].astype(f32)
-        scale = lax.rsqrt((squares(a) + squares(b)) * (1.0 / channels) + 1e-06)
+        ssq = jnp.sum(a * a, axis=1, keepdims=True) + jnp.sum(b * b, axis=1, keepdims=True)
+        edge_scale = lax.rsqrt(ssq * (1.0 / channels) + 1e-06)
         for h, v in enumerate((a, b)):
-            v = jnp.where(inside[side], activate(v, scale, gains[h]), 0.0)
-            if side == 0:
-                put_rows(h, pl.ds(0, LEAD), v[EDGE - LEAD :])
-            else:
-                put_rows(h, pl.ds(LEAD + positions, LEAD), v[:LEAD])
+            v = jax.nn.gelu(v * edge_scale * gains[h], approximate=True)
+            edges[h].append(v.T.astype(bf16))
+    for h in range(2):
+        core = c if h == 0 else 1 - c
+        mean = jnp.dot(act[h], mean_of, preferred_element_type=f32)
+        for side in range(2):
+            mean = mean + jnp.dot(edges[h][side], edge_means[side], preferred_element_type=f32)
+        win[pl.ds(pl.multiple_of(core * half, 16), half), :] = mean.astype(bf16)
 
     stage2(E)
-
-    total = jnp.zeros((count, half), f32)
+    own_y(KV)
+    own_y(Q)
+
+    middle = slice(halo_width * count, (halo_width + 1) * count)
+    total = jnp.dot(sig[0], mean_of[:, middle], preferred_element_type=f32)
     for t in range(taps):
         local[1 + t].wait()
-        for h in range(2):
-            window = pooled_rows(h, LEAD + t - halo_width).astype(bf16)
-            core = c if h == 0 else 1 - c
-            rows = pl.ds(pl.multiple_of(core * half, 16), half)
-            total = total + jnp.dot(window, conv_buf[t, rows, :], preferred_element_type=f32)
-
-    @pl.loop(0, positions // block)
-    def _(i):
-        rows = pl.ds(pl.multiple_of(i * block, block), block)
-        put = pl.ds(pl.multiple_of(LEAD + i * block, 8), block)
-        put_rows(0, put, sig[0, rows, :].astype(f32))
-
-    pooled = (total + pooled_rows(0, LEAD)).astype(bf16)
-
+        total = total + jnp.dot(
+            conv_buf[t], win[:, t * count : (t + 1) * count], preferred_element_type=f32
+        )
+    pooled = total.astype(bf16)
+
+    stage2(KV)
     stage3(E)
-    own_y(KV)
-    own_y(Q)
 
     swaps = []
     for k, (dz, same) in enumerate(owners()):
         owner = owner_of(dz, same)
         arrived(E, dz, same)
-        part[0, owner] = jnp.dot(pooled, e_buf[owner], preferred_element_type=f32).astype(bf16)
+        part[0, owner] = jnp.dot(e_buf[owner], pooled, preferred_element_type=f32).astype(bf16)
         swaps.append(remote(part.at[0, owner], other.at[0, owner], ex_sem, (0, k), partner))
-    stage2(KV)
     stage2(Q)
+    own_y(O)
     for copy in swaps:
         copy.wait_recv()
-    square = jnp.zeros((count, 1), f32)
+    square = jnp.zeros((1, count), f32)
     for b in range(n):
         v = (part[0, b].astype(f32) + other[0, b].astype(f32)).astype(bf16)
         emb[b] = v
-        square = square + squares(v.astype(f32))
+        v = v.astype(f32)
+        square = square + jnp.sum(v * v, axis=0, keepdims=True)
     scale = lax.rsqrt(square * (1.0 / (n * width)) + 1e-06)
-    for b in range(n):
-        normed[b] = (emb[b].astype(f32) * scale * attn_gain[pl.ds(b, 1), :]).astype(bf16)
+    for b in range(0, n, 2):
+        columns = slice(b * width, (b + 2) * width)
+        v = jnp.concatenate([emb[b], emb[b + 1]], axis=0).astype(f32) * scale
+        normed[:, columns] = (v.T * attn_gain[:, columns]).astype(bf16)
 
     stage3(KV)
     stage3(Q)
-    own_y(O)
 
     passed = []
     for k, (dz, same) in enumerate(owners()):
@@ -468,9 +475,11 @@
     for copy in passed:
         copy.wait_recv()
     own_tokens = pl.ds(pl.multiple_of(c * (count // 2), 16), count // 2)
-    kv = jnp.zeros((count // 2, k_buf.shape[2]), f32)
-    for b in range(n):
-        kv = kv + jnp.dot(normed[b, own_tokens, :], k_buf[b], preferred_element_type=f32)
+    kv = jnp.dot(
+        normed[own_tokens, :],
+        k_buf[...].reshape(n * width, k_buf.shape[2]),
+        preferred_element_type=f32,
+    )
 
     def kv_at(owner):
         return kv_all.at[owner, own_tokens]
@@ -484,11 +493,11 @@
     kv_copies["y", 0] = remote(mine, mine, kv_sem, (0,), y_peer)
     across = [remote(mine, mine, kp_sem, (0,), partner)]
 
-    queries = jnp.zeros((count, q_cols), f32)
     for dz, same in owners():
         arrived(Q, dz, same)
-    for b in range(n):
-        queries = queries + jnp.dot(normed[b], q_buf[b], preferred_element_type=f32)
+    queries = jnp.dot(
+        normed[...], q_buf[...].reshape(n * width, q_cols), preferred_element_type=f32
+    )
     queries = (queries * (DK**-0.5)).astype(bf16)
 
     for dz in range(1, nz):
@@ -506,6 +515,7 @@
 
     everything = kv_all[...].reshape(n * count, kv_all.shape[2])
     keys, values = everything[:, :DK], everything[:, DK:]
+    att = []
     for h in range(heads):
         scores = lax.dot_general(
             queries[:, h * DK : (h + 1) * DK],
@@ -516,18 +526,15 @@
         weights = jnp.exp(scores - jnp.max(scores, axis=1, keepdims=True))
         norm = jnp.sum(weights, axis=1, keepdims=True)
         mixed = jnp.dot(weights.astype(bf16), values, preferred_element_type=f32)
-        att[h] = (mixed / norm).astype(bf16)
+        att.append((mixed / norm).astype(bf16))
+    att = jnp.concatenate(att, axis=1)
 
     stage3(O)
     swaps = []
     for k, (dz, same) in enumerate(owners()):
         owner = owner_of(dz, same)
         arrived(O, dz, same)
-        acc = jnp.zeros((count, width), f32)
-        for h in range(heads):
-            acc = acc + jnp.dot(
-                att[h], o_buf[owner, h * DV : (h + 1) * DV, :], preferred_element_type=f32
-            )
+        acc = lax.dot_general(o_buf[owner], att, over_rows, preferred_element_type=f32)
         part[1, owner] = acc.astype(bf16)
         swaps.append(remote(part.at[1, owner], other.at[1, owner], ex_sem, (1, k), partner))
     for copy in swaps:
@@ -538,20 +545,22 @@
     token_of = lax.broadcasted_iota(jnp.int32, (rows_n, count), 1) // PAIR_POOL
     pool = jnp.where(row_of == token_of, 1.0 / PAIR_POOL, 0.0).astype(bf16)
     features = pair_w.shape[0]
-    projected = jnp.zeros((rows_n, 2 * features), f32)
-    for b in range(n):
-        v = emb[b].astype(f32) + (part[1, b].astype(f32) + other[1, b].astype(f32))
-        emb[b] = v.astype(bf16)
-        pair_pool = jnp.dot(pool, emb[b], preferred_element_type=f32).astype(bf16)
-        projected = projected + jnp.dot(pair_pool, rowcol[b], preferred_element_type=f32)
+    for b in range(0, n, 2):
+        columns = slice(b * width, (b + 2) * width)
+        pair = [
+            emb[k].astype(f32) + (part[1, k].astype(f32) + other[1, k].astype(f32))
+            for k in (b, b + 1)
+        ]
+        normed[:, columns] = jnp.concatenate(pair, axis=0).T.astype(bf16)
+    pair_pool = jnp.dot(pool, normed[...], preferred_element_type=f32).astype(bf16)
+    projected = jnp.dot(pair_pool, rowcol[...], preferred_element_type=f32)
     projected = projected.astype(bf16).astype(f32)
     cols[s] = projected[:, features:]
     col_copies = []
     for d in range(1, n):
         to = {"seq": (s + d) % n}
         col_copies.append(remote(cols.at[s], cols.at[s], col_sem, (d,), to))
-    for b in range(n):
-        tokens_out[b] = emb[b, own_tokens, :]
+    tokens_out[...] = normed[own_tokens, :]
     for copy in col_copies:
         copy.wait_recv()
     row_part = projected[:, None, :features]
@@ -597,27 +606,28 @@
     tokens, pair = pl.pallas_call(
         functools.partial(fused_kernel, taps, heads),
         out_shape=(
-            jax.ShapeDtypeStruct((n, count // 2, width), bf16),
+            jax.ShapeDtypeStruct((count // 2, n * width), bf16),
             jax.ShapeDtypeStruct((rows_n, rows_n * n // 2, features), bf16),
         ),
         in_specs=[any_spec, any_spec, vmem, any_spec, vmem]
         + [any_spec, any_spec, any_spec, vmem, vmem],
         out_specs=(vmem, vmem),
         scratch_shapes=[
-            pltpu.VMEM((2, positions, half), bf16),
-            pltpu.VMEM((2, pl.cdiv(half, 128), positions + 2 * LEAD, 128), f32),
+            pltpu.VMEM((2, half, positions), bf16),
+            pltpu.VMEM((2, half, positions), bf16),
+            pltpu.VMEM((2 * half, taps * count), bf16),
+            pltpu.VMEM((EDGE, half), bf16),
             pltpu.VMEM((2, 2, EDGE, half), bf16),
-            pltpu.VMEM((taps, channels, half), bf16),
-            pltpu.VMEM((n, half, width), bf16),
+            pltpu.VMEM((taps, half, channels), bf16),
+            pltpu.VMEM((n, width, half), bf16),
             pltpu.VMEM((n, width, q_cols), bf16),
             pltpu.VMEM((n, width, kv_cols), bf16),
-            pltpu.VMEM((n, heads * DV, width), bf16),
-            pltpu.VMEM((2, n, count, width), bf16),
-            pltpu.VMEM((2, n, count, width), bf16),
-            pltpu.VMEM((n, count, width), bf16),
-            pltpu.VMEM((n, count, width), bf16),
+            pltpu.VMEM((n, width, heads * DV), bf16),
+            pltpu.VMEM((2, n, width, count), bf16),
+            pltpu.VMEM((2, n, width, count), bf16),
+            pltpu.VMEM((n, width, count), bf16),
+            pltpu.VMEM((count, n * width), bf16),
             pltpu.VMEM((n, count, kv_cols), bf16),
-            pltpu.VMEM((heads, count, DV), bf16),
             pltpu.VMEM((n, rows_n, features), f32),
             pltpu.VMEM((rows_n, rows_n * n // 2, features), f32),
             dma((5 + taps,)),
@@ -633,18 +643,18 @@
             collective_id=0, has_side_effects=True, vmem_limit_bytes=60 * 1024 * 1024
         ),
     )(
-        signal,
-        conv_weight,
+        signal.T,
+        jnp.swapaxes(conv_weight, 1, 2),
         conv_gain.reshape(2, half),
-        embed_weight,
-        attn_gain.reshape(n, width),
+        embed_weight.T,
+        attn_gain.reshape(1, n * width),
         query_weight,
         keyvalue_weight,
-        output_weight,
-        rowcol_weight.reshape(n, width, 2 * features),
+        output_weight.T,
+        rowcol_weight,
         pair_weight,
     )
-    return jnp.transpose(tokens, (1, 0, 2)).reshape(count // 2, n * width), pair
+    return tokens, pair
 
 
 def fits(mesh):

time: 141 us -> 137 us (0.972)
  local copies, waits for them, and re-layouts: 26.8 us -> 5.75 us
  Pallas kernels: 112 us -> 130 us
    unnamed x5 -> x2, local copies, waits for them, and re-layouts: 22 us -> 3.09 us
    pallas_call x1, Pallas kernels: 112 us -> 130 us  [on_device_fused(): pl.pallas_call(functools.partial(fused_kernel, taps, heads), out_shape=(j...]
where the time goes in v2:
time: 137 us
  Pallas kernels  130 us (95%)
  local copies, waits for them, and re-layouts  5.75 us (4%)
    pallas_call x1, Pallas kernels, on_device_fused(): pl.pallas_call(functools.partial(fused_kernel, taps, heads), out_shape=(j...  130 us
    unnamed x2, local copies, waits for them, and re-layouts  3.09 us

profile of v2, /device:TPU:0, one launch (start us, length us, event | category | flops | bytes accessed | tf_op | source)
XLA Modules:
  0.0 136.8 jit_solution(12319386881280420881)
XLA Ops:
  0.6 1.4 reshape.10.conv_gain
  2.0 1.3 reshape.11.attn_gain
  3.3 130.4 %shard_map.113 = (bf16[64,1536]{1,0:T(8,128)(2,1)}, bf16[8,32,128]{2,1,0:T(8,128)(2,1)}) custom-call(bf16[704,512]{1,0:T(8,128)(2,1)} %bitcast.5, bf16[5,704,1408]{2,1,0:T(8,128)(2,1)} %bitcast.4, f32[2,704]{1,0:T(2,128)} %reshape.10.conv_gain, bf16[192,704]{1,0:T(8,128)(2,1)} %bitcast.7, f32[1,1536]{1,0:T(1,128)} %reshape.11.attn_gain, ...), custom_call_target="tpu_custom_call" | custom-call | tf_op jit(solution)/shard_map/pallas_call | solution.py:606
  133.7 1.6 %copy.14 = bf16[64,1536]{1,0:T(8,128)(2,1)} copy(bf16[64,1536]{1,0:T(8,128)(2,1)} %get-tuple-element.4) | data formatting | bytes 393216
  135.3 1.5 %copy.15 = bf16[8,32,128]{2,1,0:T(8,128)(2,1)} copy(bf16[8,32,128]{2,1,0:T(8,128)(2,1)} %get-tuple-element.5) | data formatting | bytes 131072

commit v3 on v2

--- a/solution.py
+++ b/solution.py
@@ -251,6 +251,7 @@
     partner = {"col": 1 - c}
     y_peer = {"seq": seq_of(z, 1 - y)}
     x_peer = {"grp": 1 - x}
+    z_next = {"seq": seq_of(z_to(1), y)}
 
     local = [pltpu.make_async_copy(signal, sig.at[0], loc_sem.at[0])]
     local[0].start()
@@ -276,7 +277,6 @@
 
     pieces = [(embed_w, e_at), (kv_own, k_at), (q_own, q_at), (o_own, o_at)]
     E, KV, Q, O = range(4)
-    whole = (O,)
     for t in range(taps):
         local.append(pltpu.make_async_copy(conv_w.at[t], conv_buf.at[t], loc_sem.at[1 + t]))
     for w, (own, at) in enumerate(pieces):
@@ -310,12 +310,7 @@
 
     def along_z(w):
         own, at = pieces[w]
-        for dz in range(1, nz):
-            to = {"seq": seq_of(z_to(dz), y)}
-            if w in whole:
-                send(w, ("z", dz), dz, own, at(s), to)
-            else:
-                send(w, ("z", dz), dz, rows_half(own, x), rows_half(at(s), x), to)
+        send(w, ("z", 1), 1, rows_half(own, x), rows_half(at(s), x), z_next)
 
     def own_y(w):
         own, at = pieces[w]
@@ -326,9 +321,10 @@
         for dz in range(1, nz):
             copies[w, ("z", dz)].wait_recv()
             ref = rows_half(at(seq_of(z_from(dz), y)), x)
+            if dz + 1 < nz:
+                send(w, ("z", dz + 1), dz + 1, ref, ref, z_next)
             send(w, ("y", dz), nz + dz, ref, ref, y_peer)
-            if w not in whole:
-                send(w, ("x", dz), 2 * nz + dz, ref, ref, x_peer)
+            send(w, ("x", dz), 2 * nz + dz, ref, ref, x_peer)
 
     def stage3(w):
         _, at = pieces[w]
@@ -354,7 +350,7 @@
                 copies[w, ("y", 0)].wait_recv()
         elif not same:
             copies[w, ("xy", dz)].wait_recv()
-        elif w not in whole:
+        else:
             copies[w, ("x", dz)].wait_recv()
 
     along_z(E)

time: 137 us -> 117 us (0.85)
  Pallas kernels: 130 us -> 111 us
    pallas_call x1, Pallas kernels: 130 us -> 111 us  [on_device_fused(): pl.pallas_call(functools.partial(fused_kernel, taps, heads), out_shape=(j...]
where the time goes in v3:
time: 117 us
  Pallas kernels  111 us (95%)
  local copies, waits for them, and re-layouts  5.75 us (5%)
    pallas_call x1, Pallas kernels, on_device_fused(): pl.pallas_call(functools.partial(fused_kernel, taps, heads), out_shape=(j...  111 us
    unnamed x2, local copies, waits for them, and re-layouts  3.09 us

profile of v3, /device:TPU:0, one launch (start us, length us, event | category | flops | bytes accessed | tf_op | source)
XLA Modules:
  0.0 116.9 jit_solution(6878798773770621213)
XLA Ops:
  0.6 1.4 %reshape.10.conv_gain = f32[2,704]{1,0:T(2,128)} reshape(f32[1408]{0:T(1024)} %param.12) | data formatting | bytes 11264 | tf_op jit(solution)/shard_map/reshape | solution.py:644
  2.0 1.3 %reshape.11.attn_gain = f32[1,1536]{1,0:T(1,128)} reshape(f32[1536]{0:T(1024)} %param.14) | data formatting | bytes 12288 | tf_op jit(solution)/shard_map/reshape | solution.py:646
  3.3 110.5 %shard_map.113 = (bf16[64,1536]{1,0:T(8,128)(2,1)}, bf16[8,32,128]{2,1,0:T(8,128)(2,1)}) custom-call(bf16[704,512]{1,0:T(8,128)(2,1)} %bitcast.5, bf16[5,704,1408]{2,1,0:T(8,128)(2,1)} %bitcast.4, f32[2,704]{1,0:T(2,128)} %reshape.10.conv_gain, bf16[192,704]{1,0:T(8,128)(2,1)} %bitcast.7, f32[1,1536]{1,0:T(1,128)} %reshape.11.attn_gain, ...), custom_call_target="tpu_custom_call" | custom-call | tf_op jit(solution)/shard_map/pallas_call | solution.py:602
  113.8 1.6 %copy.14 = bf16[64,1536]{1,0:T(8,128)(2,1)} copy(bf16[64,1536]{1,0:T(8,128)(2,1)} %get-tuple-element.4) | data formatting | bytes 393216
  115.4 1.5 %copy.15 = bf16[8,32,128]{2,1,0:T(8,128)(2,1)} copy(bf16[8,32,128]{2,1,0:T(8,128)(2,1)} %get-tuple-element.5) | data formatting | bytes 131072
